TPU v7x, 1024 devices: a whole 4x4x32 slice. The times are simulated.
1024 devices in a mesh: grp: 16 (over z_lo, core), dev: 64 (over y, x, z_hi).
Axes of the slice: x: 4, y: 4, z: 32 (z_hi: 4, z_lo: 8; z = z_hi * 8 + z_lo), core: 2. Of those that a mesh axis runs over, the one named last changes fastest.
Arguments:
- amplitudes: float32 [2, 65536, 128], P(None, ('grp', 'dev')), may hold values from -6 to 6
- couplings: float32 [2, 12, 128, 128], replicated, may hold values from -1 to 1, as said below
- block_index: int32 [4096], P(('grp', 'dev')), may hold values from 0 to 11
- bond_map: int32 [10], replicated, may hold values from 0 to 6
- bond_strength: float32 [10], replicated, may hold values from 0.05 to 0.5
- drive_amplitude: float32 [4, 10], replicated, may hold values from 0.05 to 0.5
Outputs:
- new_amplitudes: float32 [2, 65536, 128], P(None, ('grp', 'dev'))
Inputs may be any that keep to these rules, and one draw needn't show every extreme that they name: couplings[0][k] is symmetric and couplings[1][k] antisymmetric, so each listed coupling is Hermitian.
All inputs are finite; a program needn't handle non-finite values.
Results may differ from a plain program's by a relative error of at most 0.00007.
Values sent between devices are 32-bit elements; how exact they have to be, the bound alone decides.
No kernel may reach another device: no remote copies, remote signals or barrier semaphores. Data moves between devices by JAX's collectives and lax.ppermute only.
A program may use at most 32 MiB of HBM per device.

v0:
```python
import jax
import jax.numpy as jnp
from jax import lax
from jax.sharding import PartitionSpec as P

BROWS = 16


STEP_SIZE = 0.5
HIGHEST = lax.Precision.HIGHEST


def swapped(shard, axis, distance):
    return lax.ppermute(shard, axis, [(i, i ^ 1 << distance) for i in range(lax.axis_size(axis))])


def spin_count(number):
    return number.bit_length() - 1


def flip_group(real_part, imag_part, bit_now):
    return swapped((real_part, imag_part), "grp", bit_now)


def coupled(real_part, imag_part, table, row_kind, kinds):
    row_count, col_count = real_part.shape
    product = jnp.dot(
        jnp.concatenate([real_part, imag_part], 0),
        table,
        precision=HIGHEST,
        preferred_element_type=jnp.float32,
    )
    extent = kinds * col_count
    left_part = product[:, :extent]
    right_part = product[:, extent:]
    all_real = left_part[:row_count] - right_part[row_count:]
    all_imag = left_part[row_count:] + right_part[:row_count]
    select = (row_kind[:, None] == jnp.arange(kinds, dtype=jnp.int32)[None, :]).astype(jnp.float32)[
        :, :, None
    ]
    out_real = jnp.sum(all_real.reshape(row_count, kinds, col_count) * select, axis=1)
    out_imag = jnp.sum(all_imag.reshape(row_count, kinds, col_count) * select, axis=1)
    return (out_real, out_imag)


def evaluate_field(
    real_part, imag_part, table, row_kind, kinds, bond_map, bond_strength, drive_row
):
    out_real, out_imag = coupled(real_part, imag_part, table, row_kind, kinds)
    row_count, col_count = real_part.shape
    dev_bits = spin_count(lax.axis_size("dev"))
    grp_bits = spin_count(lax.axis_size("grp"))
    columns = jnp.arange(col_count, dtype=jnp.int32)
    for lead_spin in range(dev_bits + grp_bits):
        target = bond_map[lead_spin]
        shuffle = jnp.bitwise_xor(columns, jnp.left_shift(jnp.int32(1), target))
        sign_col = (1 - 2 * jnp.bitwise_and(jnp.right_shift(columns, target), 1)).astype(
            jnp.float32
        )[None, :]
        if lead_spin < dev_bits:
            part_real, part_imag = swapped((real_part, imag_part), "dev", lead_spin)
            sign_lead = (
                1 - 2 * jnp.bitwise_and(jnp.right_shift(lax.axis_index("dev"), lead_spin), 1)
            ).astype(jnp.float32)
        else:
            part_real, part_imag = flip_group(real_part, imag_part, lead_spin - dev_bits)
            sign_lead = (
                1
                - 2
                * jnp.bitwise_and(jnp.right_shift(lax.axis_index("grp"), lead_spin - dev_bits), 1)
            ).astype(jnp.float32)
        strength = bond_strength[lead_spin]
        drive_now = drive_row[lead_spin]
        out_real = (
            out_real
            + strength * (sign_lead * sign_col * real_part + jnp.take(part_real, shuffle, axis=1))
            + drive_now * part_real
        )
        out_imag = (
            out_imag
            + strength * (sign_lead * sign_col * imag_part + jnp.take(part_imag, shuffle, axis=1))
            + drive_now * part_imag
        )
    return (out_imag, -out_real)


def runge_kutta(real_part, imag_part, evaluate):
    half_step = 0.5 * STEP_SIZE
    slope_one = evaluate(0, real_part, imag_part)
    slope_two = evaluate(
        1, real_part + half_step * slope_one[0], imag_part + half_step * slope_one[1]
    )
    slope_three = evaluate(
        2, real_part + half_step * slope_two[0], imag_part + half_step * slope_two[1]
    )
    slope_four = evaluate(
        3, real_part + STEP_SIZE * slope_three[0], imag_part + STEP_SIZE * slope_three[1]
    )
    factor = STEP_SIZE / 6.0
    new_real = real_part + factor * (
        slope_one[0] + 2.0 * slope_two[0] + 2.0 * slope_three[0] + slope_four[0]
    )
    new_imag = imag_part + factor * (
        slope_one[1] + 2.0 * slope_two[1] + 2.0 * slope_three[1] + slope_four[1]
    )
    return (new_real, new_imag)


def body(amplitudes, couplings, block_index, bond_map, bond_strength, drive_amplitude):
    kinds = couplings.shape[1]
    col_count = couplings.shape[2]
    table_real = jnp.transpose(couplings[0], (2, 0, 1)).reshape(col_count, kinds * col_count)
    table_imag = jnp.transpose(couplings[1], (2, 0, 1)).reshape(col_count, kinds * col_count)
    table = jnp.concatenate([table_real, table_imag], 1)
    real_part = amplitudes[0]
    imag_part = amplitudes[1]
    row_count = real_part.shape[0]
    row_kind = jnp.repeat(block_index, BROWS, total_repeat_length=row_count)

    def evaluate(section, first, second):
        return evaluate_field(
            first, second, table, row_kind, kinds, bond_map, bond_strength, drive_amplitude[section]
        )

    new_real, new_imag = runge_kutta(real_part, imag_part, evaluate)
    return jnp.stack([new_real, new_imag])


def solution(mesh):
    in_specs = (P(None, ("grp", "dev"), None), P(), P(("grp", "dev")), P(), P(), P())
    out_specs = P(None, ("grp", "dev"), None)
    return jax.shard_map(body, mesh=mesh, in_specs=in_specs, out_specs=out_specs, check_vma=False)
```

profile of v0, /device:TPU:1, one launch (start us, length us, event | category | flops | bytes accessed | tf_op | source)
XLA Modules:
  0.0 631.9 jit_solution(4912484508871734299)
XLA Ops:
  0.9 16.3 %collective-permute-start.10 = (f32[64,128]{0,1:T(8,128)S(1)}, f32[64,128]{0,1:T(8,128)S(1)}, u32[]{:S(2)}, u32[]{:S(2)}) collective-permute-start(f32[64,128]{0,1:T(8,128)S(1)} %bitcast.968), channel_id=1, source_target_pairs={{0,1},{1,0},{2,3},{3,2},{4,5},{5,4},{6,7},{7,6},{8,9},{9,8},{10,11... | collective-permute-start | bytes 98312 | tf_op jit(solution)/shard_map/ppermute | solution.py:14
  17.1 19.1 %collective-permute-start.11 = (f32[64,128]{0,1:T(8,128)S(1)}, f32[64,128]{0,1:T(8,128)S(1)}, u32[]{:S(2)}, u32[]{:S(2)}) collective-permute-start(f32[64,128]{0,1:T(8,128)S(1)} %bitcast.969), channel_id=1, source_target_pairs={{0,2},{1,3},{2,0},{3,1},{4,6},{5,7},{6,4},{7,5},{8,10},{9,11},{10,... | collective-permute-start | bytes 98312 | tf_op jit(solution)/shard_map/ppermute | solution.py:14
  96.3 8.2 %collective-permute-start = (f32[64,128]{0,1:T(8,128)S(1)}, f32[64,128]{0,1:T(8,128)S(1)}, u32[]{:S(2)}, u32[]{:S(2)}) collective-permute-start(f32[64,128]{0,1:T(8,128)S(1)} %bitcast.980), channel_id=1, source_target_pairs={{0,1},{1,0},{2,3},{3,2},{4,5},{5,4},{6,7},{7,6},{8,9},{9,8},{10,11... | collective-permute-start | bytes 98312 | tf_op jit(solution)/shard_map/ppermute | solution.py:14
  104.5 5.8 collective-permute-start.1
  142.1 8.6 %collective-permute-start.9 = (f32[64,128]{0,1:T(8,128)S(1)}, f32[64,128]{0,1:T(8,128)S(1)}, u32[]{:S(2)}, u32[]{:S(2)}) collective-permute-start(f32[64,128]{0,1:T(8,128)S(1)} %bitcast.989), channel_id=1, source_target_pairs={{0,512},{64,576},{128,640},{192,704},{256,768},{320,832},{384,896}... | collective-permute-start | bytes 98312 | tf_op jit(solution)/shard_map/ppermute | solution.py:14
  150.8 14.4 %multiply_add_fusion.4 = (f32[64,128]{0,1:T(8,128)S(1)}, f32[64,128]{0,1:T(8,128)}) fusion(f32[1,64,128]{1,2,0:T(8,128)S(1)} %copy.25, f32[64,128]{0,1:T(8,128)S(1)} %collective-permute-done.19, f32[]{:T(128)} %bitcast.51, f32[128,64]{1,0:T(8,128)} %gather_fusion.19, pred[128]{0:T(512)(128)(4,1)S(1)} %get-tuple-element.114, f32[128]{0:T(128)} %get-tuple-element.124, ...), kind=kLoop, calls=%fused_computation.450 | loop fusion | flops 598016 | bytes 825680 | tf_op jit(solution)/shard_map/add | solution.py:91
  175.2 15.5 %collective-permute-start.21 = (f32[64,128]{0,1:T(8,128)S(1)}, f32[64,128]{0,1:T(8,128)S(1)}, u32[]{:S(2)}, u32[]{:S(2)}) collective-permute-start(f32[64,128]{0,1:T(8,128)S(1)} %get-tuple-element.36), channel_id=1, source_target_pairs={{0,2},{1,3},{2,0},{3,1},{4,6},{5,7},{6,4},{7,5},{8,10},{9,11},{10,... | collective-permute-start | bytes 98312 | tf_op jit(solution)/shard_map/ppermute | solution.py:14
  194.1 5.6 collective-permute-start.23
  203.3 14.1 %multiply_add_fusion.5 = (f32[64,128]{0,1:T(8,128)}, f32[64,128]{0,1:T(8,128)}) fusion(f32[1,64,128]{1,2,0:T(8,128)S(1)} %copy.24, f32[64,128]{0,1:T(8,128)S(1)} %collective-permute-done.9, f32[]{:T(128)} %bitcast.51, f32[128,64]{1,0:T(8,128)S(1)} %gather_fusion.9, pred[128]{0:T(512)(128)(4,1)S(1)} %get-tuple-element.114, f32[128]{0:T(128)} %get-tuple-element.124, ...), kind=kLoop, calls=%fused_computation.451 | loop fusion | flops 589824 | bytes 825680 | tf_op jit(solution)/shard_map/add | solution.py:91
  219.8 5.7 collective-permute-start.25
  241.8 8.2 %collective-permute-start.30 = (f32[64,128]{0,1:T(8,128)}, f32[64,128]{0,1:T(8,128)S(1)}, u32[]{:S(2)}, u32[]{:S(2)}) collective-permute-start(f32[64,128]{0,1:T(8,128)} %get-tuple-element.34), channel_id=1, source_target_pairs={{0,1},{1,0},{2,3},{3,2},{4,5},{5,4},{6,7},{7,6},{8,9},{9,8},{10,11... | collective-permute-start | bytes 98312 | tf_op jit(solution)/shard_map/ppermute | solution.py:14
  250.0 5.8 collective-permute-start.31
  291.6 7.5 %collective-permute-start.39 = (f32[64,128]{0,1:T(8,128)}, f32[64,128]{0,1:T(8,128)S(1)}, u32[]{:S(2)}, u32[]{:S(2)}) collective-permute-start(f32[64,128]{0,1:T(8,128)} %get-tuple-element.34), channel_id=1, source_target_pairs={{0,512},{64,576},{128,640},{192,704},{256,768},{320,832},{384,896}... | collective-permute-start | bytes 98312 | tf_op jit(solution)/shard_map/ppermute | solution.py:14
  299.2 14.5 %multiply_add_fusion.3 = (f32[64,128]{0,1:T(8,128)}, f32[64,128]{0,1:T(8,128)}) fusion(f32[1,64,128]{1,2,0:T(8,128)S(1)} %copy.24, f32[64,128]{0,1:T(8,128)} %collective-permute-done.29, f32[]{:T(128)} %bitcast.81, f32[128,64]{1,0:T(8,128)} %gather_fusion.29, pred[128]{0:T(512)(128)(4,1)S(1)} %get-tuple-element.114, f32[64,128]{0,1:T(8,128)S(1)} %copy-done.5, ...), kind=kLoop, calls=%fused_computation.449 | loop fusion | flops 589824 | bytes 825680 | tf_op jit(solution)/shard_map/add | solution.py:94
  323.8 15.5 %collective-permute-start.51 = (f32[64,128]{0,1:T(8,128)}, f32[64,128]{0,1:T(8,128)S(1)}, u32[]{:S(2)}, u32[]{:S(2)}) collective-permute-start(f32[64,128]{0,1:T(8,128)} %get-tuple-element.30), channel_id=1, source_target_pairs={{0,2},{1,3},{2,0},{3,1},{4,6},{5,7},{6,4},{7,5},{8,10},{9,11},{10,... | collective-permute-start | bytes 98312 | tf_op jit(solution)/shard_map/ppermute | solution.py:14
  342.8 5.6 collective-permute-start.53
  352.0 14.3 %multiply_add_fusion.2 = (f32[64,128]{0,1:T(8,128)}, f32[64,128]{0,1:T(8,128)}) fusion(f32[1,64,128]{1,2,0:T(8,128)S(1)} %copy.25, f32[64,128]{0,1:T(8,128)S(1)} %collective-permute-done.39, f32[]{:T(128)} %bitcast.81, f32[128,64]{1,0:T(8,128)S(1)} %gather_fusion.39, pred[128]{0:T(512)(128)(4,1)S(1)} %get-tuple-element.114, ...), kind=kLoop, calls=%fused_computation.448 | loop fusion | flops 598016 | bytes 825680 | tf_op jit(solution)/shard_map/add | solution.py:94
  368.7 5.8 collective-permute-start.55
  390.8 8.2 %collective-permute-start.40 = (f32[64,128]{0,1:T(8,128)}, f32[64,128]{0,1:T(8,128)S(1)}, u32[]{:S(2)}, u32[]{:S(2)}) collective-permute-start(f32[64,128]{0,1:T(8,128)} %get-tuple-element.32), channel_id=1, source_target_pairs={{0,1},{1,0},{2,3},{3,2},{4,5},{5,4},{6,7},{7,6},{8,9},{9,8},{10,11... | collective-permute-start | bytes 98312 | tf_op jit(solution)/shard_map/ppermute | solution.py:14
  399.0 5.8 collective-permute-start.41
  440.4 7.5 %collective-permute-start.49 = (f32[64,128]{0,1:T(8,128)}, f32[64,128]{0,1:T(8,128)S(1)}, u32[]{:S(2)}, u32[]{:S(2)}) collective-permute-start(f32[64,128]{0,1:T(8,128)} %get-tuple-element.32), channel_id=1, source_target_pairs={{0,512},{64,576},{128,640},{192,704},{256,768},{320,832},{384,896}... | collective-permute-start | bytes 98312 | tf_op jit(solution)/shard_map/ppermute | solution.py:14
  447.9 14.5 %multiply_add_fusion = (f32[64,128]{0,1:T(8,128)S(1)}, f32[64,128]{0,1:T(8,128)}) fusion(f32[1,64,128]{1,2,0:T(8,128)S(1)} %copy.25, f32[64,128]{0,1:T(8,128)} %collective-permute-done.59, f32[]{:T(128)} %bitcast.111, f32[128,64]{1,0:T(8,128)} %gather_fusion.59, pred[128]{0:T(512)(128)(4,1)S(1)} %get-tuple-element.114, f32[64,128]{0,1:T(8,128)} %get-tuple-element.30, ...), kind=kLoop, calls=%fused_computation.446 | loop fusion | flops 598016 | bytes 825680 | tf_op jit(solution)/shard_map/add | solution.py:97
  472.6 15.5 %collective-permute-start.61 = (f32[64,128]{0,1:T(8,128)S(1)}, f32[64,128]{0,1:T(8,128)S(1)}, u32[]{:S(2)}, u32[]{:S(2)}) collective-permute-start(f32[64,128]{0,1:T(8,128)S(1)} %get-tuple-element.28), channel_id=1, source_target_pairs={{0,2},{1,3},{2,0},{3,1},{4,6},{5,7},{6,4},{7,5},{8,10},{9,11},{10,... | collective-permute-start | bytes 98312 | tf_op jit(solution)/shard_map/ppermute | solution.py:14
  491.5 5.6 collective-permute-start.63
  501.9 13.7 %multiply_add_fusion.1 = (f32[64,128]{0,1:T(8,128)S(1)}, f32[64,128]{0,1:T(8,128)S(1)}) fusion(f32[1,64,128]{1,2,0:T(8,128)S(1)} %copy.24, f32[64,128]{0,1:T(8,128)S(1)} %collective-permute-done.49, f32[]{:T(128)} %bitcast.111, f32[128,64]{1,0:T(8,128)} %gather_fusion.49, pred[128]{0:T(512)(128)(4,1)S(1)} %get-tuple-element.114, ...), kind=kLoop, calls=%fused_computation.447 | loop fusion | flops 589824 | bytes 825680 | tf_op jit(solution)/shard_map/add | solution.py:97
  515.6 5.8 collective-permute-start.65
  537.3 8.2 %collective-permute-start.70 = (f32[64,128]{0,1:T(8,128)S(1)}, f32[64,128]{0,1:T(8,128)S(1)}, u32[]{:S(2)}, u32[]{:S(2)}) collective-permute-start(f32[64,128]{0,1:T(8,128)S(1)} %get-tuple-element.26), channel_id=1, source_target_pairs={{0,1},{1,0},{2,3},{3,2},{4,5},{5,4},{6,7},{7,6},{8,9},{9,8},{10,11... | collective-permute-start | bytes 98312 | tf_op jit(solution)/shard_map/ppermute | solution.py:14
  545.4 5.8 collective-permute-start.71
  561.9 7.7 %collective-permute-done.71 = f32[64,128]{0,1:T(8,128)S(1)} collective-permute-done((f32[64,128]{0,1:T(8,128)S(1)}, f32[64,128]{0,1:T(8,128)S(1)}, u32[]{:S(2)}, u32[]{:S(2)}) %collective-permute-start.71) | collective-permute-done | bytes 32800 | tf_op jit(solution)/shard_map/ppermute | solution.py:14
  579.8 9.1 %collective-permute-start.79 = (f32[64,128]{0,1:T(8,128)S(1)}, f32[64,128]{0,1:T(8,128)S(1)}, u32[]{:S(2)}, u32[]{:S(2)}) collective-permute-start(f32[64,128]{0,1:T(8,128)S(1)} %get-tuple-element.26), channel_id=1, source_target_pairs={{0,512},{64,576},{128,640},{192,704},{256,768},{320,832},{384,896}... | collective-permute-start | bytes 98312 | tf_op jit(solution)/shard_map/ppermute | solution.py:14
  605.4 12.9 %fusion.57 = f32[1,64,128]{1,2,0:T(8,128)S(1)} fusion(f32[64,128]{0,1:T(8,128)S(1)} %copy.21, f32[128,64]{1,0:T(8,128)S(1)} %gather_fusion.69, f32[128,64]{1,0:T(8,128)S(1)} %gather_fusion.68, f32[128,64]{1,0:T(8,128)S(1)} %gather_fusion.67, f32[128,64]{1,0:T(8,128)S(1)} %gather_fusion.66, f32[128,64]{1,0:T(8,128)S(1)} %gather_fusion.65, ...), kind=kLoop, calls=%fused_computation.166 | loop fusion | flops 630784 | bytes 891216 | tf_op jit(solution)/shard_map/stack | solution.py:126
  618.3 12.9 %fusion.23 = f32[1,64,128]{1,2,0:T(8,128)S(1)} fusion(f32[64,128]{0,1:T(8,128)S(1)} %copy.22, f32[128,64]{1,0:T(8,128)S(1)} %gather_fusion.79, f32[128,64]{1,0:T(8,128)S(1)} %gather_fusion.78, f32[128,64]{1,0:T(8,128)S(1)} %gather_fusion.77, f32[128,64]{1,0:T(8,128)S(1)} %gather_fusion.76, f32[128,64]{1,0:T(8,128)S(1)} %gather_fusion.75, ...), kind=kLoop, calls=%fused_computation.122 | loop fusion | flops 638976 | bytes 891216 | tf_op jit(solution)/shard_map/stack | solution.py:126
  (452 shorter events, 299.7 us)
Async XLA Ops:
  0.9 74.9 %collective-permute-start.10 = (f32[64,128]{0,1:T(8,128)S(1)}, f32[64,128]{0,1:T(8,128)S(1)}, u32[]{:S(2)}, u32[]{:S(2)}) collective-permute-start(f32[64,128]{0,1:T(8,128)S(1)} %bitcast.968), channel_id=1, source_target_pairs={{0,1},{1,0},{2,3},{3,2},{4,5},{5,4},{6,7},{7,6},{8,9},{9,8},{10,11... | collective-permute-start | bytes 98312 | tf_op jit(solution)/shard_map/ppermute | solution.py:14
  17.1 63.1 %collective-permute-start.11 = (f32[64,128]{0,1:T(8,128)S(1)}, f32[64,128]{0,1:T(8,128)S(1)}, u32[]{:S(2)}, u32[]{:S(2)}) collective-permute-start(f32[64,128]{0,1:T(8,128)S(1)} %bitcast.969), channel_id=1, source_target_pairs={{0,2},{1,3},{2,0},{3,1},{4,6},{5,7},{6,4},{7,5},{8,10},{9,11},{10,... | collective-permute-start | bytes 98312 | tf_op jit(solution)/shard_map/ppermute | solution.py:14
  36.2 48.3 %collective-permute-start.12 = (f32[64,128]{0,1:T(8,128)S(1)}, f32[64,128]{0,1:T(8,128)S(1)}, u32[]{:S(2)}, u32[]{:S(2)}) collective-permute-start(f32[64,128]{0,1:T(8,128)S(1)} %bitcast.970), channel_id=1, source_target_pairs={{0,4},{1,5},{2,6},{3,7},{4,0},{5,1},{6,2},{7,3},{8,12},{9,13},{10,... | collective-permute-start | bytes 98312 | tf_op jit(solution)/shard_map/ppermute | solution.py:14
  39.4 47.9 %collective-permute-start.13 = (f32[64,128]{0,1:T(8,128)S(1)}, f32[64,128]{0,1:T(8,128)S(1)}, u32[]{:S(2)}, u32[]{:S(2)}) collective-permute-start(f32[64,128]{0,1:T(8,128)S(1)} %bitcast.971), channel_id=1, source_target_pairs={{0,8},{1,9},{2,10},{3,11},{4,12},{5,13},{6,14},{7,15},{8,0},{9,1},... | collective-permute-start | bytes 98312 | tf_op jit(solution)/shard_map/ppermute | solution.py:14
  43.7 46.6 %collective-permute-start.14 = (f32[64,128]{0,1:T(8,128)S(1)}, f32[64,128]{0,1:T(8,128)S(1)}, u32[]{:S(2)}, u32[]{:S(2)}) collective-permute-start(f32[64,128]{0,1:T(8,128)S(1)} %bitcast.972), channel_id=1, source_target_pairs={{0,16},{1,17},{2,18},{3,19},{4,20},{5,21},{6,22},{7,23},{8,24},{9,... | collective-permute-start | bytes 98312 | tf_op jit(solution)/shard_map/ppermute | solution.py:14
  129.5 39.5 %collective-permute-start.5 = (f32[64,128]{0,1:T(8,128)S(1)}, f32[64,128]{0,1:T(8,128)S(1)}, u32[]{:S(2)}, u32[]{:S(2)}) collective-permute-start(f32[64,128]{0,1:T(8,128)S(1)} %bitcast.985), channel_id=1, source_target_pairs={{0,32},{1,33},{2,34},{3,35},{4,36},{5,37},{6,38},{7,39},{8,40},{9,... | collective-permute-start | bytes 98312 | tf_op jit(solution)/shard_map/ppermute | solution.py:14
  132.6 42.6 %collective-permute-start.6 = (f32[64,128]{0,1:T(8,128)S(1)}, f32[64,128]{0,1:T(8,128)S(1)}, u32[]{:S(2)}, u32[]{:S(2)}) collective-permute-start(f32[64,128]{0,1:T(8,128)S(1)} %bitcast.986), channel_id=1, source_target_pairs={{0,64},{64,0},{128,192},{192,128},{256,320},{320,256},{384,448},{4... | collective-permute-start | bytes 98312 | tf_op jit(solution)/shard_map/ppermute | solution.py:14
  136.7 54.7 %collective-permute-start.7 = (f32[64,128]{0,1:T(8,128)S(1)}, f32[64,128]{0,1:T(8,128)S(1)}, u32[]{:S(2)}, u32[]{:S(2)}) collective-permute-start(f32[64,128]{0,1:T(8,128)S(1)} %bitcast.987), channel_id=1, source_target_pairs={{0,128},{64,192},{128,0},{192,64},{256,384},{320,448},{384,256},{4... | collective-permute-start | bytes 98312 | tf_op jit(solution)/shard_map/ppermute | solution.py:14
  138.7 55.5 %collective-permute-start.8 = (f32[64,128]{0,1:T(8,128)S(1)}, f32[64,128]{0,1:T(8,128)S(1)}, u32[]{:S(2)}, u32[]{:S(2)}) collective-permute-start(f32[64,128]{0,1:T(8,128)S(1)} %bitcast.988), channel_id=1, source_target_pairs={{0,256},{64,320},{128,384},{192,448},{256,0},{320,64},{384,128},{4... | collective-permute-start | bytes 98312 | tf_op jit(solution)/shard_map/ppermute | solution.py:14
  142.1 58.3 %collective-permute-start.9 = (f32[64,128]{0,1:T(8,128)S(1)}, f32[64,128]{0,1:T(8,128)S(1)}, u32[]{:S(2)}, u32[]{:S(2)}) collective-permute-start(f32[64,128]{0,1:T(8,128)S(1)} %bitcast.989), channel_id=1, source_target_pairs={{0,512},{64,576},{128,640},{192,704},{256,768},{320,832},{384,896}... | collective-permute-start | bytes 98312 | tf_op jit(solution)/shard_map/ppermute | solution.py:14
  169.0 50.8 %collective-permute-start.20 = (f32[64,128]{0,1:T(8,128)S(1)}, f32[64,128]{0,1:T(8,128)S(1)}, u32[]{:S(2)}, u32[]{:S(2)}) collective-permute-start(f32[64,128]{0,1:T(8,128)S(1)} %get-tuple-element.36), channel_id=1, source_target_pairs={{0,1},{1,0},{2,3},{3,2},{4,5},{5,4},{6,7},{7,6},{8,9},{9,8},{10,11... | collective-permute-start | bytes 98312 | tf_op jit(solution)/shard_map/ppermute | solution.py:14
  175.2 50.3 %collective-permute-start.21 = (f32[64,128]{0,1:T(8,128)S(1)}, f32[64,128]{0,1:T(8,128)S(1)}, u32[]{:S(2)}, u32[]{:S(2)}) collective-permute-start(f32[64,128]{0,1:T(8,128)S(1)} %get-tuple-element.36), channel_id=1, source_target_pairs={{0,2},{1,3},{2,0},{3,1},{4,6},{5,7},{6,4},{7,5},{8,10},{9,11},{10,... | collective-permute-start | bytes 98312 | tf_op jit(solution)/shard_map/ppermute | solution.py:14
  191.4 38.5 %collective-permute-start.22 = (f32[64,128]{0,1:T(8,128)S(1)}, f32[64,128]{0,1:T(8,128)S(1)}, u32[]{:S(2)}, u32[]{:S(2)}) collective-permute-start(f32[64,128]{0,1:T(8,128)S(1)} %get-tuple-element.36), channel_id=1, source_target_pairs={{0,4},{1,5},{2,6},{3,7},{4,0},{5,1},{6,2},{7,3},{8,12},{9,13},{10,... | collective-permute-start | bytes 98312 | tf_op jit(solution)/shard_map/ppermute | solution.py:14
  194.1 38.5 %collective-permute-start.23 = (f32[64,128]{0,1:T(8,128)S(1)}, f32[64,128]{0,1:T(8,128)S(1)}, u32[]{:S(2)}, u32[]{:S(2)}) collective-permute-start(f32[64,128]{0,1:T(8,128)S(1)} %get-tuple-element.36), channel_id=1, source_target_pairs={{0,8},{1,9},{2,10},{3,11},{4,12},{5,13},{6,14},{7,15},{8,0},{9,1},... | collective-permute-start | bytes 98312 | tf_op jit(solution)/shard_map/ppermute | solution.py:14
  277.8 39.8 %collective-permute-start.35 = (f32[64,128]{0,1:T(8,128)}, f32[64,128]{0,1:T(8,128)S(1)}, u32[]{:S(2)}, u32[]{:S(2)}) collective-permute-start(f32[64,128]{0,1:T(8,128)} %get-tuple-element.34), channel_id=1, source_target_pairs={{0,32},{1,33},{2,34},{3,35},{4,36},{5,37},{6,38},{7,39},{8,40},{9,... | collective-permute-start | bytes 98312 | tf_op jit(solution)/shard_map/ppermute | solution.py:14
  281.0 42.8 %collective-permute-start.36 = (f32[64,128]{0,1:T(8,128)}, f32[64,128]{0,1:T(8,128)S(1)}, u32[]{:S(2)}, u32[]{:S(2)}) collective-permute-start(f32[64,128]{0,1:T(8,128)} %get-tuple-element.34), channel_id=1, source_target_pairs={{0,64},{64,0},{128,192},{192,128},{256,320},{320,256},{384,448},{4... | collective-permute-start | bytes 98312 | tf_op jit(solution)/shard_map/ppermute | solution.py:14
  285.2 54.9 %collective-permute-start.37 = (f32[64,128]{0,1:T(8,128)}, f32[64,128]{0,1:T(8,128)S(1)}, u32[]{:S(2)}, u32[]{:S(2)}) collective-permute-start(f32[64,128]{0,1:T(8,128)} %get-tuple-element.34), channel_id=1, source_target_pairs={{0,128},{64,192},{128,0},{192,64},{256,384},{320,448},{384,256},{4... | collective-permute-start | bytes 98312 | tf_op jit(solution)/shard_map/ppermute | solution.py:14
  287.1 55.7 %collective-permute-start.38 = (f32[64,128]{0,1:T(8,128)}, f32[64,128]{0,1:T(8,128)S(1)}, u32[]{:S(2)}, u32[]{:S(2)}) collective-permute-start(f32[64,128]{0,1:T(8,128)} %get-tuple-element.34), channel_id=1, source_target_pairs={{0,256},{64,320},{128,384},{192,448},{256,0},{320,64},{384,128},{4... | collective-permute-start | bytes 98312 | tf_op jit(solution)/shard_map/ppermute | solution.py:14
  291.6 57.5 %collective-permute-start.39 = (f32[64,128]{0,1:T(8,128)}, f32[64,128]{0,1:T(8,128)S(1)}, u32[]{:S(2)}, u32[]{:S(2)}) collective-permute-start(f32[64,128]{0,1:T(8,128)} %get-tuple-element.34), channel_id=1, source_target_pairs={{0,512},{64,576},{128,640},{192,704},{256,768},{320,832},{384,896}... | collective-permute-start | bytes 98312 | tf_op jit(solution)/shard_map/ppermute | solution.py:14
  317.6 51.1 %collective-permute-start.50 = (f32[64,128]{0,1:T(8,128)}, f32[64,128]{0,1:T(8,128)S(1)}, u32[]{:S(2)}, u32[]{:S(2)}) collective-permute-start(f32[64,128]{0,1:T(8,128)} %get-tuple-element.30), channel_id=1, source_target_pairs={{0,1},{1,0},{2,3},{3,2},{4,5},{5,4},{6,7},{7,6},{8,9},{9,8},{10,11... | collective-permute-start | bytes 98312 | tf_op jit(solution)/shard_map/ppermute | solution.py:14
  323.8 50.7 %collective-permute-start.51 = (f32[64,128]{0,1:T(8,128)}, f32[64,128]{0,1:T(8,128)S(1)}, u32[]{:S(2)}, u32[]{:S(2)}) collective-permute-start(f32[64,128]{0,1:T(8,128)} %get-tuple-element.30), channel_id=1, source_target_pairs={{0,2},{1,3},{2,0},{3,1},{4,6},{5,7},{6,4},{7,5},{8,10},{9,11},{10,... | collective-permute-start | bytes 98312 | tf_op jit(solution)/shard_map/ppermute | solution.py:14
  340.1 38.9 %collective-permute-start.52 = (f32[64,128]{0,1:T(8,128)}, f32[64,128]{0,1:T(8,128)S(1)}, u32[]{:S(2)}, u32[]{:S(2)}) collective-permute-start(f32[64,128]{0,1:T(8,128)} %get-tuple-element.30), channel_id=1, source_target_pairs={{0,4},{1,5},{2,6},{3,7},{4,0},{5,1},{6,2},{7,3},{8,12},{9,13},{10,... | collective-permute-start | bytes 98312 | tf_op jit(solution)/shard_map/ppermute | solution.py:14
  342.8 38.9 %collective-permute-start.53 = (f32[64,128]{0,1:T(8,128)}, f32[64,128]{0,1:T(8,128)S(1)}, u32[]{:S(2)}, u32[]{:S(2)}) collective-permute-start(f32[64,128]{0,1:T(8,128)} %get-tuple-element.30), channel_id=1, source_target_pairs={{0,8},{1,9},{2,10},{3,11},{4,12},{5,13},{6,14},{7,15},{8,0},{9,1},... | collective-permute-start | bytes 98312 | tf_op jit(solution)/shard_map/ppermute | solution.py:14
  426.7 39.7 %collective-permute-start.45 = (f32[64,128]{0,1:T(8,128)}, f32[64,128]{0,1:T(8,128)S(1)}, u32[]{:S(2)}, u32[]{:S(2)}) collective-permute-start(f32[64,128]{0,1:T(8,128)} %get-tuple-element.32), channel_id=1, source_target_pairs={{0,32},{1,33},{2,34},{3,35},{4,36},{5,37},{6,38},{7,39},{8,40},{9,... | collective-permute-start | bytes 98312 | tf_op jit(solution)/shard_map/ppermute | solution.py:14
  429.8 42.8 %collective-permute-start.46 = (f32[64,128]{0,1:T(8,128)}, f32[64,128]{0,1:T(8,128)S(1)}, u32[]{:S(2)}, u32[]{:S(2)}) collective-permute-start(f32[64,128]{0,1:T(8,128)} %get-tuple-element.32), channel_id=1, source_target_pairs={{0,64},{64,0},{128,192},{192,128},{256,320},{320,256},{384,448},{4... | collective-permute-start | bytes 98312 | tf_op jit(solution)/shard_map/ppermute | solution.py:14
  433.9 54.9 %collective-permute-start.47 = (f32[64,128]{0,1:T(8,128)}, f32[64,128]{0,1:T(8,128)S(1)}, u32[]{:S(2)}, u32[]{:S(2)}) collective-permute-start(f32[64,128]{0,1:T(8,128)} %get-tuple-element.32), channel_id=1, source_target_pairs={{0,128},{64,192},{128,0},{192,64},{256,384},{320,448},{384,256},{4... | collective-permute-start | bytes 98312 | tf_op jit(solution)/shard_map/ppermute | solution.py:14
  435.9 55.7 %collective-permute-start.48 = (f32[64,128]{0,1:T(8,128)}, f32[64,128]{0,1:T(8,128)S(1)}, u32[]{:S(2)}, u32[]{:S(2)}) collective-permute-start(f32[64,128]{0,1:T(8,128)} %get-tuple-element.32), channel_id=1, source_target_pairs={{0,256},{64,320},{128,384},{192,448},{256,0},{320,64},{384,128},{4... | collective-permute-start | bytes 98312 | tf_op jit(solution)/shard_map/ppermute | solution.py:14
  440.4 58.1 %collective-permute-start.49 = (f32[64,128]{0,1:T(8,128)}, f32[64,128]{0,1:T(8,128)S(1)}, u32[]{:S(2)}, u32[]{:S(2)}) collective-permute-start(f32[64,128]{0,1:T(8,128)} %get-tuple-element.32), channel_id=1, source_target_pairs={{0,512},{64,576},{128,640},{192,704},{256,768},{320,832},{384,896}... | collective-permute-start | bytes 98312 | tf_op jit(solution)/shard_map/ppermute | solution.py:14
  466.4 49.2 %collective-permute-start.60 = (f32[64,128]{0,1:T(8,128)S(1)}, f32[64,128]{0,1:T(8,128)S(1)}, u32[]{:S(2)}, u32[]{:S(2)}) collective-permute-start(f32[64,128]{0,1:T(8,128)S(1)} %get-tuple-element.28), channel_id=1, source_target_pairs={{0,1},{1,0},{2,3},{3,2},{4,5},{5,4},{6,7},{7,6},{8,9},{9,8},{10,11... | collective-permute-start | bytes 98312 | tf_op jit(solution)/shard_map/ppermute | solution.py:14
  472.6 48.8 %collective-permute-start.61 = (f32[64,128]{0,1:T(8,128)S(1)}, f32[64,128]{0,1:T(8,128)S(1)}, u32[]{:S(2)}, u32[]{:S(2)}) collective-permute-start(f32[64,128]{0,1:T(8,128)S(1)} %get-tuple-element.28), channel_id=1, source_target_pairs={{0,2},{1,3},{2,0},{3,1},{4,6},{5,7},{6,4},{7,5},{8,10},{9,11},{10,... | collective-permute-start | bytes 98312 | tf_op jit(solution)/shard_map/ppermute | solution.py:14
  488.8 37.0 %collective-permute-start.62 = (f32[64,128]{0,1:T(8,128)S(1)}, f32[64,128]{0,1:T(8,128)S(1)}, u32[]{:S(2)}, u32[]{:S(2)}) collective-permute-start(f32[64,128]{0,1:T(8,128)S(1)} %get-tuple-element.28), channel_id=1, source_target_pairs={{0,4},{1,5},{2,6},{3,7},{4,0},{5,1},{6,2},{7,3},{8,12},{9,13},{10,... | collective-permute-start | bytes 98312 | tf_op jit(solution)/shard_map/ppermute | solution.py:14
  558.9 42.3 %collective-permute-start.75 = (f32[64,128]{0,1:T(8,128)S(1)}, f32[64,128]{0,1:T(8,128)S(1)}, u32[]{:S(2)}, u32[]{:S(2)}) collective-permute-start(f32[64,128]{0,1:T(8,128)S(1)} %get-tuple-element.26), channel_id=1, source_target_pairs={{0,32},{1,33},{2,34},{3,35},{4,36},{5,37},{6,38},{7,39},{8,40},{9,... | collective-permute-start | bytes 98312 | tf_op jit(solution)/shard_map/ppermute | solution.py:14
  (130 other events, 4138.1 us)
where the time goes:
time: 638 us; the launch traced here: 632 us
  starting transfers between devices  386 us (61%)
  other arithmetic  130 us (20%)
  local copies, waits for them, and re-layouts  91.2 us (14%)
  between operations  9.05 us (1%)
  matrix products  7.9 us (1%)
  waiting for transfers between devices  7.87 us (1%)
    ppermute x80, starting transfers between devices, swapped(): lax.ppermute(shard, axis, [(i, i ^ 1 << distance) for i in range(lax.axis...  386 us
    gather x40, local copies, waits for them, and re-layouts, evaluate_field(): jnp.take(part_real, shuffle, axis=1)  36.8 us
    gather x40, local copies, waits for them, and re-layouts, evaluate_field(): jnp.take(part_imag, shuffle, axis=1)  35.5 us
    another operation x3, other arithmetic, body(): return jnp.stack([new_real, new_imag])  25.8 us
    add x1, other arithmetic, runge_kutta(): real_part + half_step * slope_two[0]  14.5 us
    add x1, other arithmetic, runge_kutta(): imag_part + STEP_SIZE * slope_three[1]  14.5 us
    add x1, other arithmetic, runge_kutta(): imag_part + half_step * slope_one[1]  14.4 us
    add x1, other arithmetic, runge_kutta(): imag_part + half_step * slope_two[1]  14.3 us
  transfers between devices with their start and end apart: 80, of which 1 were waited for; matrix products, arithmetic and copies ran while one was open for 32% of the time, Pallas kernels for 0%

commit v1 on v0

v1 whole, which is shorter than its diff:
```python
import functools

import jax
import jax.numpy as jnp
from jax import lax
from jax.experimental import pallas as pl
from jax.experimental.pallas import tpu as pltpu
from jax.sharding import Mesh, PartitionSpec as P

BROWS = 16
STEP_SIZE = 0.5

ROWS = 64
COLS = 128
KINDS = 12
LEAD = 10
UNITS = 16
PAYLOAD = 136
TWO = 2 * COLS

ORDER = sorted(range(UNITS), key=lambda u: (u.bit_count(), u))
PLANE = {2: 0, 3: 1, 4: 2, 5: 3}
ROW_BIT = {0: 0, 1: 1, 6: 2, 7: 3, 8: 4, 9: 5}
GROUPS = ((5, 5, 5), (6, 5), (5,), (1,))


def prep_kernel(index_ref, amp_ref, out_ref):
    out_ref[:, 0, 0:COLS] = amp_ref[0]
    out_ref[:, 0, COLS:TWO] = amp_ref[1]
    block = lax.broadcasted_iota(jnp.int32, (ROWS, COLS), 0) // BROWS
    kind = jnp.zeros((ROWS, COLS), jnp.int32)
    for q in range(ROWS // BROWS):
        kind = jnp.where(block == q, index_ref[q], kind)
    out_ref[:, 0, TWO : TWO + COLS] = kind.astype(jnp.float32)


def pack_kernel(in_ref, out_ref):
    real = in_ref[:, 0, 0:COLS]
    imag = in_ref[:, 0, COLS:TWO]
    kind = in_ref[:, 0, TWO : TWO + COLS]
    row = lax.broadcasted_iota(jnp.int32, (ROWS, COLS), 0)
    lane = lax.broadcasted_iota(jnp.int32, (ROWS, COLS), 1)
    kinds = jnp.sum(jnp.where(row == lane, kind, 0.0), axis=0, keepdims=True)
    kinds = jnp.broadcast_to(kinds, (PAYLOAD - 2 * ROWS, COLS))
    for u in range(UNITS):
        out_ref[u, 0:ROWS] = real
        out_ref[u, ROWS : 2 * ROWS] = imag
        out_ref[u, 2 * ROWS :] = kinds


def unpack_kernel(in_ref, out_ref):
    out_ref[0] = in_ref[:, 0, 0:COLS]
    out_ref[1] = in_ref[:, 0, COLS:TWO]


def flip_rows(field, bit):
    if bit >= 3:
        step = 1 << (bit - 3)
        tiles = field.reshape(8 // (2 * step), 2, step, 8, COLS)
        return jnp.concatenate([tiles[:, 1:], tiles[:, :1]], axis=1).reshape(ROWS, COLS)
    tiles = field.reshape(8, 8, COLS)
    step = 1 << bit
    if bit == 2:
        return pltpu.roll(tiles, 4, 1).reshape(ROWS, COLS)
    row = lax.broadcasted_iota(jnp.int32, (8, 8, COLS), 1)
    up = pltpu.roll(tiles, 8 - step, 1)
    down = pltpu.roll(tiles, step, 1)
    return jnp.where((row & step) == 0, up, down).reshape(ROWS, COLS)


def step_kernel(
    bond_ref,
    strength_ref,
    drive_ref,
    gathered_ref,
    couplings_ref,
    out_ref,
    order_ref,
    states,
    kinds,
    diag_ref,
    sign_ref,
    lane_ref,
    high_w,
    low_w,
    high_x,
    low_x,
    lead_ref,
    total,
):
    own = lax.axis_index("plane")
    for p, u in enumerate(ORDER):
        order_ref[p] = jnp.int32(u)

    def split(k, carry):
        real = couplings_ref[0, k]
        imag = couplings_ref[1, k]
        for r, row in enumerate(((real, -imag), (imag, real))):
            for c, block in enumerate(row):
                rows = pl.ds(pl.multiple_of(k * TWO + r * COLS, COLS), COLS)
                high = block.astype(jnp.bfloat16)
                high_w[rows, c * COLS : (c + 1) * COLS] = high
                low_w[rows, c * COLS : (c + 1) * COLS] = (
                    block - high.astype(jnp.float32)
                ).astype(jnp.bfloat16)
        return carry

    lax.fori_loop(0, KINDS, split, 0)

    row = lax.broadcasted_iota(jnp.int32, (ROWS, COLS), 0)
    lane = lax.broadcasted_iota(jnp.int32, (ROWS, COLS), 1)

    diag = jnp.zeros((ROWS, COLS), jnp.float32)
    for a in range(LEAD):
        target = bond_ref[a]
        lane_ref[a] = jnp.bitwise_xor(lane[:8], jnp.left_shift(jnp.int32(1), target))
        sign = (1 - 2 * jnp.bitwise_and(jnp.right_shift(lane, target), 1)).astype(jnp.float32)
        sign = strength_ref[a] * sign
        if a in PLANE:
            sign_ref[PLANE[a]] = sign[:8]
        else:
            lead = (1 - 2 * jnp.bitwise_and(jnp.right_shift(row, ROW_BIT[a]), 1)).astype(jnp.float32)
            diag = diag + lead * sign
    diag_ref[...] = diag

    def arrive(u, carry):
        there = jnp.bitwise_xor(u, own)
        states[0, u, 0] = gathered_ref[there, 0:ROWS]
        states[0, u, 1] = gathered_ref[there, ROWS : 2 * ROWS]
        listed = jnp.broadcast_to(gathered_ref[there, 2 * ROWS : 2 * ROWS + 1], (ROWS, COLS))
        kind = jnp.sum(jnp.where(row == lane, listed, 0.0), axis=1, keepdims=True)
        kinds[u] = jnp.broadcast_to(kind, (ROWS, COLS)).astype(jnp.bfloat16)
        return carry

    lax.fori_loop(0, UNITS, arrive, 0)

    def scatter(section, p):
        u = order_ref[p]
        rows = pl.ds(pl.multiple_of(p * ROWS, ROWS), ROWS)
        kind = kinds[u]
        for part in range(2):
            x = states[section, u, part]
            high = x.astype(jnp.bfloat16)
            low = (x - high.astype(jnp.float32)).astype(jnp.bfloat16)
            zero = jnp.zeros_like(high)
            for k in range(KINDS):
                chosen = kind == jnp.bfloat16(k)
                at = k * TWO + part * COLS
                high_x[rows, at : at + COLS] = jnp.where(chosen, high, zero)
                low_x[rows, at : at + COLS] = jnp.where(chosen, low, zero)
        weight = jnp.zeros((8, COLS), jnp.float32)
        here = jnp.bitwise_xor(u, own)
        for bit in range(4):
            sign = (1 - 2 * jnp.bitwise_and(jnp.right_shift(here, bit), 1)).astype(jnp.float32)
            weight = weight + sign * sign_ref[bit]
        weight = (diag_ref[...].reshape(8, 8, COLS) + weight[None]).reshape(ROWS, COLS)
        for part in range(2):
            x = states[section, u, part]
            out = weight * x
            for a in range(LEAD):
                if a in PLANE:
                    y = states[section, jnp.bitwise_xor(u, 1 << PLANE[a]), part]
                else:
                    y = x
                where = jnp.broadcast_to(lane_ref[a][None], (8, 8, COLS)).reshape(ROWS, COLS)
                shuffled = jnp.take_along_axis(y, where, axis=1)
                term = strength_ref[a] * shuffled + drive_ref[section, a] * y
                if a not in PLANE:
                    term = flip_rows(term, ROW_BIT[a])
                out = out + term
            lead_ref[p, part] = out

    def combine(section, first, count):
        rows = pl.ds(pl.multiple_of(first * ROWS, ROWS), count * ROWS)
        dot = functools.partial(jnp.dot, preferred_element_type=jnp.float32)
        out = dot(high_x[rows, :], high_w[...])
        out = out + dot(low_x[rows, :], high_w[...])
        out = out + dot(high_x[rows, :], low_w[...])
        ahead = (0.5, 0.5, 1.0, 0.0)[section] * STEP_SIZE
        for i in range(count):
            u = order_ref[first + i]
            h_real = out[i * ROWS : (i + 1) * ROWS, :COLS] + lead_ref[first + i, 0]
            h_imag = out[i * ROWS : (i + 1) * ROWS, COLS:] + lead_ref[first + i, 1]
            if section < 3:
                states[section + 1, u, 0] = states[0, u, 0] + ahead * h_imag
                states[section + 1, u, 1] = states[0, u, 1] - ahead * h_real
            if i == 0:
                share = (1.0, 2.0, 2.0, 1.0)[section] * STEP_SIZE / 6.0

                def keep():
                    if section == 0:
                        total[0] = states[0, 0, 0] + share * h_imag
                        total[1] = states[0, 0, 1] - share * h_real
                    elif section < 3:
                        total[0] = total[0] + share * h_imag
                        total[1] = total[1] - share * h_real
                    else:
                        out_ref[:, 0, 0:COLS] = total[0] + share * h_imag
                        out_ref[:, 0, COLS:TWO] = total[1] - share * h_real

                if isinstance(first, int):
                    if first == 0:
                        keep()
                else:
                    pl.when(first == 0)(keep)

    for section, groups in enumerate(GROUPS):

        def one(p, carry, section=section):
            scatter(section, p)
            return carry

        lax.fori_loop(0, sum(groups), one, 0)
        if len(set(groups)) == 1 and len(groups) > 1:

            def many(c, carry, section=section, count=groups[0]):
                combine(section, c * count, count)
                return carry

            lax.fori_loop(0, len(groups), many, 0)
        else:
            first = 0
            for count in groups:
                combine(section, first, count)
                first += count


def body(amplitudes, couplings, block_index, bond_map, bond_strength, drive_amplitude):
    f32 = jnp.float32
    vmem = pl.BlockSpec(memory_space=pltpu.VMEM)
    smem = pl.BlockSpec(memory_space=pltpu.SMEM)
    line = ("grp", "far")
    sent = pl.pallas_call(
        prep_kernel,
        out_shape=jax.ShapeDtypeStruct((ROWS, 1, TWO + COLS), f32),
        in_specs=[smem, vmem],
        out_specs=vmem,
    )(block_index, amplitudes)
    held = lax.all_to_all(sent, line, 0, 0, tiled=True)
    copies = pl.pallas_call(
        pack_kernel,
        out_shape=jax.ShapeDtypeStruct((UNITS, PAYLOAD, COLS), f32),
        in_specs=[vmem],
        out_specs=vmem,
    )(held)
    gathered = lax.all_to_all(copies, "plane", 0, 0, tiled=True)
    result = pl.pallas_call(
        step_kernel,
        out_shape=jax.ShapeDtypeStruct((ROWS, 1, TWO), f32),
        in_specs=[smem, smem, smem, vmem, vmem],
        out_specs=vmem,
        scratch_shapes=[
            pltpu.SMEM((UNITS,), jnp.int32),
            pltpu.VMEM((4, UNITS, 2, ROWS, COLS), f32),
            pltpu.VMEM((UNITS, ROWS, COLS), jnp.bfloat16),
            pltpu.VMEM((ROWS, COLS), f32),
            pltpu.VMEM((4, 8, COLS), f32),
            pltpu.VMEM((LEAD, 8, COLS), jnp.int32),
            pltpu.VMEM((KINDS * TWO, TWO), jnp.bfloat16),
            pltpu.VMEM((KINDS * TWO, TWO), jnp.bfloat16),
            pltpu.VMEM((15 * ROWS, KINDS * TWO), jnp.bfloat16),
            pltpu.VMEM((15 * ROWS, KINDS * TWO), jnp.bfloat16),
            pltpu.VMEM((15, 2, ROWS, COLS), f32),
            pltpu.VMEM((2, ROWS, COLS), f32),
        ],
    )(bond_map, bond_strength, drive_amplitude, gathered, couplings)
    back = lax.all_to_all(result, line, 0, 0, tiled=True)
    return pl.pallas_call(
        unpack_kernel,
        out_shape=jax.ShapeDtypeStruct((2, ROWS, COLS), f32),
        in_specs=[vmem],
        out_specs=vmem,
    )(back)


def solution(mesh):
    names = ("grp", "plane", "far")
    split = Mesh(mesh.devices.reshape(16, 16, 4), names)
    in_specs = (P(None, names, None), P(), P(names), P(), P(), P())
    return jax.shard_map(body, mesh=split, in_specs=in_specs, out_specs=P(None, names, None), check_vma=False)
```

time: 638 us -> 150 us (0.24)
  starting transfers between devices: 386 us -> 0 us
  other arithmetic: 130 us -> 0 us
  blocking collectives: 0 us -> 112 us
  local copies, waits for them, and re-layouts: 91.2 us -> 0 us
  Pallas kernels: 0 us -> 37.9 us
  between operations: 9.05 us -> 0.01 us
  matrix products: 7.9 us -> 0 us
  waiting for transfers between devices: 7.87 us -> 0 us
    ppermute x80 -> x0, starting transfers between devices: 386 us -> none  [swapped(): lax.ppermute(shard, axis, [(i, i ^ 1 << distance) for i in range(lax.axis...]
    all_to_all x0 -> x3, blocking collectives: none -> 112 us  [the longest x1 56.6 us: body(): held = lax.all_to_all(sent, line, 0, 0, tiled=True)]
    add x6 -> x0, other arithmetic: 85.4 us -> none  [the longest x1 14.5 us: runge_kutta(): real_part + half_step * slope_two[0]]
    gather x81 -> x0, local copies, waits for them, and re-layouts: 73 us -> none  [the longest x40 36.8 us: evaluate_field(): jnp.take(part_real, shuffle, axis=1)]
    pallas_call x0 -> x4, Pallas kernels: none -> 37.9 us  [the longest x1 32.9 us: body(): pl.pallas_call(step_kernel, out_shape=jax.ShapeDtypeStruct((ROWS, 1, TWO)...]
    another operation x3 -> x0, other arithmetic: 25.8 us -> none  [body(): return jnp.stack([new_real, new_imag])]
    slice x7 -> x0, local copies, waits for them, and re-layouts: 10.3 us -> none  [the longest x3 5.6 us: evaluate_field(): drive_now = drive_row[lead_spin]]
    mul x5 -> x0, other arithmetic: 8.62 us -> none  [evaluate_field(): sign_lead * sign_col * imag_part + jnp.take(part_imag, shuffle, axis=1)]
  transfers between devices with their start and end apart: 80 -> 0, of which waited for: 1 -> 0; matrix products, arithmetic and copies ran while one was open for 32% -> 0% of each run, Pallas kernels for 0% -> 0%
where the time goes in v1:
time: 150 us
  blocking collectives  112 us (75%)
  Pallas kernels  37.9 us (25%)
    all_to_all x1, blocking collectives, body(): held = lax.all_to_all(sent, line, 0, 0, tiled=True)  56.6 us
    pallas_call x1, Pallas kernels, body(): pl.pallas_call(step_kernel, out_shape=jax.ShapeDtypeStruct((ROWS, 1, TWO)...  32.9 us
    all_to_all x1, blocking collectives, body(): back = lax.all_to_all(result, line, 0, 0, tiled=True)  31 us
    all_to_all x1, blocking collectives, body(): gathered = lax.all_to_all(copies, 'plane', 0, 0, tiled=True)  24.3 us

profile of v1, /device:TPU:1, one launch (start us, length us, event | category | flops | bytes accessed | tf_op | source)
XLA Modules:
  0.0 149.9 jit_solution(15286620302437086240)
XLA Ops:
  0.0 1.5 %shard_map.64 = f32[64,1,384]{2,1,0:T(1,128)} custom-call(s32[4]{0:T(128)} %index_ref.1, f32[2,64,128]{2,1,0:T(8,128)} %amp_ref.1), custom_call_target="tpu_custom_call" | custom-call | tf_op jit(solution)/shard_map/pallas_call | solution.py:233
  1.5 56.6 %all_to_all.15.in_ref = f32[64,1,384]{2,1,0:T(1,128)} all-to-all(f32[64,1,384]{2,1,0:T(1,128)} %shard_map.64), channel_id=1, replica_groups=mesh['grp'=16,'plane'=16,'far'=4] {'grp','far'}, dimensions={0} | all-to-all | bytes 196608 | tf_op jit(solution)/shard_map/all_to_all | solution.py:239
  58.2 2.0 %shard_map.65 = f32[16,136,128]{2,1,0:T(8,128)} custom-call(f32[64,1,384]{2,1,0:T(1,128)} %all_to_all.15.in_ref), custom_call_target="tpu_custom_call" | custom-call | tf_op jit(solution)/shard_map/pallas_call | solution.py:240
  60.2 24.3 %all_to_all.16.gathered_ref = f32[16,136,128]{2,1,0:T(8,128)} all-to-all(f32[16,136,128]{2,1,0:T(8,128)} %shard_map.65), channel_id=1, replica_groups=mesh['grp'=16,'plane'=16,'far'=4] {'plane'}, dimensions={0} | all-to-all | bytes 2228224 | tf_op jit(solution)/shard_map/all_to_all | solution.py:246
  84.5 32.9 %shard_map.66 = f32[64,1,256]{2,1,0:T(1,128)} custom-call(s32[10]{0:T(128)} %bond_ref.1, f32[10]{0:T(128)} %strength_ref.1, f32[4,10]{1,0:T(4,128)} %drive_ref.1, f32[16,136,128]{2,1,0:T(8,128)} %all_to_all.16.gathered_ref, f32[2,12,128,128]{3,2,1,0:T(8,128)} %couplings_ref.1), custom_call_target="tpu_custom_call" | custom-call | tf_op jit(solution)/shard_map/pallas_call | solution.py:247
  117.4 31.0 %all_to_all.17.in_ref = f32[64,1,256]{2,1,0:T(1,128)} all-to-all(f32[64,1,256]{2,1,0:T(1,128)} %shard_map.66), channel_id=1, replica_groups=mesh['grp'=16,'plane'=16,'far'=4] {'grp','far'}, dimensions={0} | all-to-all | bytes 131072 | tf_op jit(solution)/shard_map/all_to_all | solution.py:267
  148.4 1.5 %shard_map.67 = f32[2,64,128]{2,1,0:T(8,128)} custom-call(f32[64,1,256]{2,1,0:T(1,128)} %all_to_all.17.in_ref), custom_call_target="tpu_custom_call" | custom-call | tf_op jit(solution)/shard_map/pallas_call | solution.py:268

commit v2 on v1

v2 whole, which is shorter than its diff:
```python
import functools

import jax
import jax.numpy as jnp
from jax import lax
from jax.experimental import pallas as pl
from jax.experimental.pallas import tpu as pltpu
from jax.sharding import Mesh, PartitionSpec as P

BROWS = 16
STEP_SIZE = 0.5

ROWS = 64
COLS = 128
KINDS = 12
LEAD = 10
UNITS = 16
PAYLOAD = 136
TWO = 2 * COLS

ORDER = sorted(range(UNITS), key=lambda u: (u.bit_count(), u))
PLACE = [ORDER.index(u) for u in range(UNITS)]
PLANE = {2: 0, 3: 1, 4: 2, 5: 3}
ROW_BIT = {0: 0, 1: 1, 6: 2, 7: 3, 8: 4, 9: 5}
GROUPS = (
    (0, (0, 1, 2, 3, 4)),
    (0, (5, 6, 7, 8, 9, 10)),
    (0, (11, 12, 13, 14)),
    (1, (0, 1, 2, 3, 4)),
    (1, (5, 6, 7, 8, 9, 10)),
    (2, (0, 1, 2, 3, 4)),
    (3, (0,)),
)
MOST = 6


def prep_kernel(index_ref, amp_ref, out_ref):
    out_ref[:, 0, 0:COLS] = amp_ref[0]
    out_ref[:, 0, COLS:TWO] = amp_ref[1]
    block = lax.broadcasted_iota(jnp.int32, (ROWS, COLS), 0) // BROWS
    kind = jnp.zeros((ROWS, COLS), jnp.int32)
    for q in range(ROWS // BROWS):
        kind = jnp.where(block == q, index_ref[q], kind)
    out_ref[:, 0, TWO : TWO + COLS] = kind.astype(jnp.float32)


def pack_kernel(in_ref, out_ref):
    real = in_ref[:, 0, 0:COLS]
    imag = in_ref[:, 0, COLS:TWO]
    kind = in_ref[:, 0, TWO : TWO + COLS]
    row = lax.broadcasted_iota(jnp.int32, (ROWS, COLS), 0)
    lane = lax.broadcasted_iota(jnp.int32, (ROWS, COLS), 1)
    kinds = jnp.sum(jnp.where(row == lane, kind, 0.0), axis=0, keepdims=True)
    kinds = jnp.broadcast_to(kinds, (PAYLOAD - 2 * ROWS, COLS))
    for u in range(UNITS):
        out_ref[u, 0:ROWS] = real
        out_ref[u, ROWS : 2 * ROWS] = imag
        out_ref[u, 2 * ROWS :] = kinds


def unpack_kernel(in_ref, out_ref):
    out_ref[0] = in_ref[:, 0, 0:COLS]
    out_ref[1] = in_ref[:, 0, COLS:TWO]


def flip_rows(field, bit):
    tiles = field.reshape(2 * ROWS // 8, 8, COLS)
    if bit >= 3:
        step = 1 << (bit - 3)
        pairs = tiles.reshape(2 * ROWS // (16 * step), 2, step, 8, COLS)
        return jnp.concatenate([pairs[:, 1:], pairs[:, :1]], axis=1).reshape(2 * ROWS, COLS)
    step = 1 << bit
    if bit == 2:
        return pltpu.roll(tiles, 4, 1).reshape(2 * ROWS, COLS)
    row = lax.broadcasted_iota(jnp.int32, (2 * ROWS // 8, 8, COLS), 1)
    up = pltpu.roll(tiles, 8 - step, 1)
    down = pltpu.roll(tiles, step, 1)
    return jnp.where((row & step) == 0, up, down).reshape(2 * ROWS, COLS)


def step_kernel(
    bond_ref,
    strength_ref,
    drive_ref,
    gathered_ref,
    couplings_hbm,
    out_ref,
    couplings_ref,
    copied,
    state_one,
    state_two,
    state_three,
    state_four,
    kinds,
    diag_ref,
    sign_ref,
    lane_ref,
    high_w,
    low_w,
    high_even,
    low_even,
    high_odd,
    low_odd,
    lead_even,
    lead_odd,
    total,
):
    f32 = jnp.float32
    bf16 = jnp.bfloat16
    copy = pltpu.make_async_copy(couplings_hbm, couplings_ref, copied)
    copy.start()
    own = lax.axis_index("plane")
    states = (state_one, state_two, state_three, state_four)
    sides = ((high_even, low_even, lead_even), (high_odd, low_odd, lead_odd))

    row = lax.broadcasted_iota(jnp.int32, (ROWS, COLS), 0)
    lane = lax.broadcasted_iota(jnp.int32, (ROWS, COLS), 1)

    diag = jnp.zeros((ROWS, COLS), f32)
    for a in range(LEAD):
        target = bond_ref[a]
        lane_ref[a] = jnp.bitwise_xor(lane[:8], jnp.left_shift(jnp.int32(1), target))
        sign = (1 - 2 * jnp.bitwise_and(jnp.right_shift(lane, target), 1)).astype(f32)
        sign = strength_ref[a] * sign
        if a in PLANE:
            sign_ref[PLANE[a]] = sign[:8]
        else:
            lead = (1 - 2 * jnp.bitwise_and(jnp.right_shift(row, ROW_BIT[a]), 1)).astype(f32)
            diag = diag + lead * sign
    diag_ref[...] = diag

    ones = jnp.ones((COLS, TWO), bf16)
    for u in ORDER:
        there = jnp.bitwise_xor(own, u)
        state_one[PLACE[u]] = gathered_ref[there, 0 : 2 * ROWS]
        listed = jnp.broadcast_to(gathered_ref[there, 2 * ROWS : 2 * ROWS + 1], (ROWS, COLS))
        spread = jnp.where(row == lane, listed, 0.0).astype(bf16)
        kinds[PLACE[u]] = jnp.dot(spread, ones, preferred_element_type=f32).astype(bf16)

    def split():
        def one(k, carry):
            parts = []
            for c in range(2):
                block = couplings_ref[c, k]
                high = block.astype(bf16)
                parts.append((high, (block - high.astype(f32)).astype(bf16)))
            for at, target in ((0, high_w), (1, low_w)):
                real, imag = parts[0][at], parts[1][at]
                top = pl.ds(pl.multiple_of(k * TWO, TWO), COLS)
                low = pl.ds(pl.multiple_of(k * TWO + COLS, COLS), COLS)
                target[top, :] = jnp.concatenate([real, -imag], axis=1)
                target[low, :] = jnp.concatenate([imag, real], axis=1)
            return carry

        lax.fori_loop(0, KINDS, one, 0)

    def left(section, u, i, side):
        x = states[section][PLACE[u]]
        both = jnp.concatenate([x[:ROWS], x[ROWS:]], axis=1)
        high = both.astype(bf16)
        low = (both - high.astype(f32)).astype(bf16)
        zero = jnp.zeros_like(high)
        kind = kinds[PLACE[u]]
        rows = slice(i * ROWS, (i + 1) * ROWS)
        for k in range(KINDS):
            chosen = kind == jnp.bfloat16(k)
            side[0][rows, k * TWO : (k + 1) * TWO] = jnp.where(chosen, high, zero)
            side[1][rows, k * TWO : (k + 1) * TWO] = jnp.where(chosen, low, zero)

    def lead(section, u, i, side):
        weight = jnp.zeros((8, COLS), f32)
        here = jnp.bitwise_xor(own, u)
        for bit in range(4):
            sign = (1 - 2 * jnp.bitwise_and(jnp.right_shift(here, bit), 1)).astype(f32)
            weight = weight + sign * sign_ref[bit]
        weight = diag_ref[...].reshape(8, 8, COLS) + weight[None]
        x = states[section][PLACE[u]]
        out = (jnp.concatenate([weight, weight], axis=0) * x.reshape(16, 8, COLS)).reshape(2 * ROWS, COLS)
        for a in range(LEAD):
            y = states[section][PLACE[u ^ (1 << PLANE[a])]] if a in PLANE else x
            where = jnp.broadcast_to(lane_ref[a][None], (16, 8, COLS)).reshape(2 * ROWS, COLS)
            shuffled = jnp.take_along_axis(y, where, axis=1)
            term = strength_ref[a] * shuffled + drive_ref[section, a] * y
            out = out + (term if a in PLANE else flip_rows(term, ROW_BIT[a]))
        side[2][i] = out

    def tasks(number):
        if number >= len(GROUPS):
            return []
        section, places = GROUPS[number]
        side = sides[number % 2]
        made = []
        for i, p in enumerate(places):
            made.append(functools.partial(left, section, ORDER[p], i, side))
            made.append(functools.partial(lead, section, ORDER[p], i, side))
        return made

    def combine(number, beside):
        section, places = GROUPS[number]
        high, low, leads = sides[number % 2]
        count = len(places)
        dot = functools.partial(jnp.dot, preferred_element_type=f32)
        out = None
        done = 0
        for k in range(KINDS):
            at = slice(k * TWO, (k + 1) * TWO)
            rows = slice(0, count * ROWS)
            part = dot(high[rows, at], high_w[at, :])
            out = part if out is None else out + part
            out = out + dot(low[rows, at], high_w[at, :])
            out = out + dot(high[rows, at], low_w[at, :])
            while done * KINDS < len(beside) * (k + 1):
                beside[done]()
                done += 1
        ahead = (0.5, 0.5, 1.0, 0.0)[section] * STEP_SIZE
        share = (1.0, 2.0, 2.0, 1.0)[section] * STEP_SIZE / 6.0
        for i, p in enumerate(places):
            h_real = out[i * ROWS : (i + 1) * ROWS, :COLS] + leads[i, :ROWS]
            h_imag = out[i * ROWS : (i + 1) * ROWS, COLS:] + leads[i, ROWS:]
            if section < 3:
                states[section + 1][p, :ROWS] = state_one[p, :ROWS] + ahead * h_imag
                states[section + 1][p, ROWS:] = state_one[p, ROWS:] - ahead * h_real
            if p == 0:
                so_far = state_one[0] if section == 0 else total[...]
                new_real = so_far[:ROWS] + share * h_imag
                new_imag = so_far[ROWS:] - share * h_real
                if section < 3:
                    total[:ROWS] = new_real
                    total[ROWS:] = new_imag
                else:
                    out_ref[:, 0, 0:COLS] = new_real
                    out_ref[:, 0, COLS:TWO] = new_imag

    for task in tasks(0):
        task()
    copy.wait()
    split()
    for number in range(len(GROUPS)):
        beside = tasks(number + 1)
        early = len(beside) if number < 4 else 2 if number == 4 else 0
        combine(number, beside[:early])
        for task in beside[early:]:
            task()


def body(amplitudes, couplings, block_index, bond_map, bond_strength, drive_amplitude):
    f32 = jnp.float32
    bf16 = jnp.bfloat16
    vmem = pl.BlockSpec(memory_space=pltpu.VMEM)
    smem = pl.BlockSpec(memory_space=pltpu.SMEM)
    small = pltpu.CompilerParams(vmem_limit_bytes=4 << 20)
    line = ("grp", "far")
    sent = pl.pallas_call(
        prep_kernel,
        out_shape=jax.ShapeDtypeStruct((ROWS, 1, TWO + COLS), f32),
        in_specs=[smem, vmem],
        out_specs=vmem,
        compiler_params=small,
    )(block_index, amplitudes)
    held = lax.all_to_all(sent, line, 0, 0, tiled=True)
    copies = pl.pallas_call(
        pack_kernel,
        out_shape=jax.ShapeDtypeStruct((UNITS, PAYLOAD, COLS), f32),
        in_specs=[vmem],
        out_specs=vmem,
        compiler_params=small,
    )(held)
    gathered = lax.all_to_all(copies, "plane", 0, 0, tiled=True)
    wide = KINDS * TWO
    result = pl.pallas_call(
        step_kernel,
        out_shape=jax.ShapeDtypeStruct((ROWS, 1, TWO), f32),
        in_specs=[smem, smem, smem, vmem, pl.BlockSpec(memory_space=pl.ANY)],
        out_specs=vmem,
        scratch_shapes=[
            pltpu.VMEM((2, KINDS, COLS, COLS), f32),
            pltpu.SemaphoreType.DMA,
        ]
        + [pltpu.VMEM((n, 2 * ROWS, COLS), f32) for n in (16, 15, 11, 5)]
        + [
            pltpu.VMEM((UNITS, ROWS, TWO), bf16),
            pltpu.VMEM((ROWS, COLS), f32),
            pltpu.VMEM((4, 8, COLS), f32),
            pltpu.VMEM((LEAD, 8, COLS), jnp.int32),
            pltpu.VMEM((wide, TWO), bf16),
            pltpu.VMEM((wide, TWO), bf16),
        ]
        + [pltpu.VMEM((MOST * ROWS, wide), bf16)] * 4
        + [pltpu.VMEM((MOST, 2 * ROWS, COLS), f32)] * 2
        + [pltpu.VMEM((2 * ROWS, COLS), f32)],
        compiler_params=pltpu.CompilerParams(vmem_limit_bytes=32 << 20),
    )(bond_map, bond_strength, drive_amplitude, gathered, couplings)
    back = lax.all_to_all(result, line, 0, 0, tiled=True)
    return pl.pallas_call(
        unpack_kernel,
        out_shape=jax.ShapeDtypeStruct((2, ROWS, COLS), f32),
        in_specs=[vmem],
        out_specs=vmem,
        compiler_params=small,
    )(back)


def solution(mesh):
    names = ("grp", "plane", "far")
    split = Mesh(mesh.devices.reshape(16, 16, 4), names)
    in_specs = (P(None, names, None), P(), P(names), P(), P(), P())
    return jax.shard_map(body, mesh=split, in_specs=in_specs, out_specs=P(None, names, None), check_vma=False)
```

time: 150 us -> 130 us (0.87)
  Pallas kernels: 37.9 us -> 17 us
  local copies, waits for them, and re-layouts: 0 us -> 1.52 us
    pallas_call x1, Pallas kernels: 32.9 us -> 15.7 us  [body(): pl.pallas_call(step_kernel, out_shape=jax.ShapeDtypeStruct((ROWS, 1, TWO)...]
    pallas_call x1, Pallas kernels: 1.98 us -> 0.09 us  [body(): pl.pallas_call(pack_kernel, out_shape=jax.ShapeDtypeStruct((UNITS, PAYLOA...]
    unnamed x0 -> x12, local copies, waits for them, and re-layouts: none -> 1.52 us
where the time goes in v2:
time: 130 us
  blocking collectives  111 us (85%)
  Pallas kernels  17 us (13%)
  local copies, waits for them, and re-layouts  1.52 us (1%)
    all_to_all x1, blocking collectives, body(): held = lax.all_to_all(sent, line, 0, 0, tiled=True)  56.3 us
    all_to_all x1, blocking collectives, body(): back = lax.all_to_all(result, line, 0, 0, tiled=True)  30.7 us
    all_to_all x1, blocking collectives, body(): gathered = lax.all_to_all(copies, 'plane', 0, 0, tiled=True)  24.1 us
    pallas_call x1, Pallas kernels, body(): pl.pallas_call(step_kernel, out_shape=jax.ShapeDtypeStruct((ROWS, 1, TWO)...  15.7 us

profile of v2, /device:TPU:1, one launch (start us, length us, event | category | flops | bytes accessed | tf_op | source)
XLA Modules:
  0.0 129.8 jit_solution(1495891198598607422)
XLA Ops:
  0.0 0.0 copy-start.1
  0.0 0.8 copy-done.1
  0.8 0.0 copy-start.3
  0.8 0.7 copy-done.3
  1.5 0.6 shard_map.64
  2.1 56.3 %all_to_all.15.in_ref = f32[64,1,384]{2,1,0:T(1,128)S(1)} all-to-all(f32[64,1,384]{2,1,0:T(1,128)S(1)} %shard_map.64), channel_id=1, replica_groups=mesh['grp'=16,'plane'=16,'far'=4] {'grp','far'}, dimensions={0} | all-to-all | bytes 196608 | tf_op jit(solution)/shard_map/all_to_all | solution.py:260
  58.4 0.1 shard_map.65
  58.5 0.0 copy-start
  58.5 0.0 copy-start.2
  58.6 0.0 copy-start.4
  58.6 0.0 copy-start.5
  58.6 24.1 %all_to_all.16.gathered_ref = f32[16,136,128]{2,1,0:T(8,128)S(1)} all-to-all(f32[16,136,128]{2,1,0:T(8,128)S(1)} %shard_map.65), channel_id=1, replica_groups=mesh['grp'=16,'plane'=16,'far'=4] {'plane'}, dimensions={0} | all-to-all | bytes 2228224 | tf_op jit(solution)/shard_map/all_to_all | solution.py:268
  82.7 0.0 copy-done
  82.7 0.0 copy-done.2
  82.7 0.0 copy-done.4
  82.7 0.0 copy-done.5
  82.7 15.7 %shard_map.66 = f32[64,1,256]{2,1,0:T(1,128)S(1)} custom-call(s32[10]{0:T(128)S(1)} %copy-done.4, f32[10]{0:T(128)S(1)} %copy-done.5, f32[4,10]{1,0:T(4,128)S(1)} %copy-done.2, f32[16,136,128]{2,1,0:T(8,128)S(1)} %all_to_all.16.gathered_ref, f32[2,12,128,128]{3,2,1,0:T(8,128)S(1)} %copy-done), custom_call_target="tpu_custom_call" | custom-call | tf_op jit(solution)/shard_map/pallas_call | solution.py:270
  98.4 30.7 %all_to_all.17.in_ref = f32[64,1,256]{2,1,0:T(1,128)S(1)} all-to-all(f32[64,1,256]{2,1,0:T(1,128)S(1)} %shard_map.66), channel_id=1, replica_groups=mesh['grp'=16,'plane'=16,'far'=4] {'grp','far'}, dimensions={0} | all-to-all | bytes 131072 | tf_op jit(solution)/shard_map/all_to_all | solution.py:293
  129.1 0.7 shard_map.67
Async XLA Ops:
  0.0 0.8 copy-start.1
  0.8 0.7 copy-start.3
  58.5 24.2 %copy-start = (f32[2,12,128,128]{3,2,1,0:T(8,128)S(1)}, f32[2,12,128,128]{3,2,1,0:T(8,128)}, u32[]{:S(2)}) copy-start(f32[2,12,128,128]{3,2,1,0:T(8,128)} %couplings_hbm.1) | copy-start | bytes 4718596
  58.5 24.2 %copy-start.2 = (f32[4,10]{1,0:T(4,128)S(1)}, f32[4,10]{1,0:T(4,128)}, u32[]{:S(2)}) copy-start(f32[4,10]{1,0:T(4,128)} %drive_ref.1) | copy-start | bytes 484
  58.6 24.2 %copy-start.4 = (s32[10]{0:T(128)S(1)}, s32[10]{0:T(128)}, u32[]{:S(2)}) copy-start(s32[10]{0:T(128)} %bond_ref.1) | copy-start | bytes 124
  58.6 24.2 %copy-start.5 = (f32[10]{0:T(128)S(1)}, f32[10]{0:T(128)}, u32[]{:S(2)}) copy-start(f32[10]{0:T(128)} %strength_ref.1) | copy-start | bytes 124

commit v3 on v2

--- a/solution.py
+++ b/solution.py
@@ -1,4 +1,5 @@
 import functools
+import itertools
 
 import jax
 import jax.numpy as jnp
@@ -15,7 +16,7 @@
 KINDS = 12
 LEAD = 10
 UNITS = 16
-PAYLOAD = 136
+PAYLOAD = 2 * ROWS + 8
 TWO = 2 * COLS
 
 ORDER = sorted(range(UNITS), key=lambda u: (u.bit_count(), u))
@@ -23,18 +24,25 @@
 PLANE = {2: 0, 3: 1, 4: 2, 5: 3}
 ROW_BIT = {0: 0, 1: 1, 6: 2, 7: 3, 8: 4, 9: 5}
 GROUPS = (
-    (0, (0, 1, 2, 3, 4)),
-    (0, (5, 6, 7, 8, 9, 10)),
-    (0, (11, 12, 13, 14)),
+    (0, (0, 1, 2, 3, 4, 5, 6)),
+    (0, (7, 8, 9, 10, 11, 12, 13, 14)),
     (1, (0, 1, 2, 3, 4)),
     (1, (5, 6, 7, 8, 9, 10)),
     (2, (0, 1, 2, 3, 4)),
     (3, (0,)),
 )
-MOST = 6
-
-
-def prep_kernel(index_ref, amp_ref, out_ref):
+MOST = 8
+
+
+def prep_kernel(index_hbm, amp_hbm, out_ref, index_ref, amp_ref, copied):
+    copies = (
+        pltpu.make_async_copy(amp_hbm, amp_ref, copied.at[0]),
+        pltpu.make_async_copy(index_hbm, index_ref, copied.at[1]),
+    )
+    for copy in copies:
+        copy.start()
+    for copy in copies:
+        copy.wait()
     out_ref[:, 0, 0:COLS] = amp_ref[0]
     out_ref[:, 0, COLS:TWO] = amp_ref[1]
     block = lax.broadcasted_iota(jnp.int32, (ROWS, COLS), 0) // BROWS
@@ -97,12 +105,9 @@
     lane_ref,
     high_w,
     low_w,
-    high_even,
-    low_even,
-    high_odd,
-    low_odd,
-    lead_even,
-    lead_odd,
+    left_even,
+    left_odd,
+    lead_ref,
     total,
 ):
     f32 = jnp.float32
@@ -111,7 +116,7 @@
     copy.start()
     own = lax.axis_index("plane")
     states = (state_one, state_two, state_three, state_four)
-    sides = ((high_even, low_even, lead_even), (high_odd, low_odd, lead_odd))
+    sides = (left_even, left_odd)
 
     row = lax.broadcasted_iota(jnp.int32, (ROWS, COLS), 0)
     lane = lax.broadcasted_iota(jnp.int32, (ROWS, COLS), 1)
@@ -137,44 +142,40 @@
         spread = jnp.where(row == lane, listed, 0.0).astype(bf16)
         kinds[PLACE[u]] = jnp.dot(spread, ones, preferred_element_type=f32).astype(bf16)
 
-    def split():
-        def one(k, carry):
-            parts = []
-            for c in range(2):
-                block = couplings_ref[c, k]
-                high = block.astype(bf16)
-                parts.append((high, (block - high.astype(f32)).astype(bf16)))
-            for at, target in ((0, high_w), (1, low_w)):
-                real, imag = parts[0][at], parts[1][at]
-                top = pl.ds(pl.multiple_of(k * TWO, TWO), COLS)
-                low = pl.ds(pl.multiple_of(k * TWO + COLS, COLS), COLS)
-                target[top, :] = jnp.concatenate([real, -imag], axis=1)
-                target[low, :] = jnp.concatenate([imag, real], axis=1)
-            return carry
-
-        lax.fori_loop(0, KINDS, one, 0)
-
-    def left(section, u, i, side):
-        x = states[section][PLACE[u]]
+    def split(k):
+        parts = []
+        for c in range(2):
+            block = couplings_ref[c, k]
+            high = block.astype(bf16)
+            parts.append((high, (block - high.astype(f32)).astype(bf16)))
+        for at, target in ((0, high_w), (1, low_w)):
+            real, imag = parts[0][at], parts[1][at]
+            target[k * TWO : k * TWO + COLS] = jnp.concatenate([real, -imag], axis=1)
+            target[k * TWO + COLS : (k + 1) * TWO] = jnp.concatenate([imag, real], axis=1)
+
+    def left(section, p, i, count, side):
+        x = states[section][p]
         both = jnp.concatenate([x[:ROWS], x[ROWS:]], axis=1)
         high = both.astype(bf16)
         low = (both - high.astype(f32)).astype(bf16)
         zero = jnp.zeros_like(high)
-        kind = kinds[PLACE[u]]
+        kind = kinds[p]
         rows = slice(i * ROWS, (i + 1) * ROWS)
+        more = slice((count + i) * ROWS, (count + i + 1) * ROWS)
         for k in range(KINDS):
             chosen = kind == jnp.bfloat16(k)
-            side[0][rows, k * TWO : (k + 1) * TWO] = jnp.where(chosen, high, zero)
-            side[1][rows, k * TWO : (k + 1) * TWO] = jnp.where(chosen, low, zero)
-
-    def lead(section, u, i, side):
+            side[rows, k * TWO : (k + 1) * TWO] = jnp.where(chosen, high, zero)
+            side[more, k * TWO : (k + 1) * TWO] = jnp.where(chosen, low, zero)
+
+    def lead(section, p, i):
+        u = ORDER[p]
         weight = jnp.zeros((8, COLS), f32)
         here = jnp.bitwise_xor(own, u)
         for bit in range(4):
             sign = (1 - 2 * jnp.bitwise_and(jnp.right_shift(here, bit), 1)).astype(f32)
             weight = weight + sign * sign_ref[bit]
         weight = diag_ref[...].reshape(8, 8, COLS) + weight[None]
-        x = states[section][PLACE[u]]
+        x = states[section][p]
         out = (jnp.concatenate([weight, weight], axis=0) * x.reshape(16, 8, COLS)).reshape(2 * ROWS, COLS)
         for a in range(LEAD):
             y = states[section][PLACE[u ^ (1 << PLANE[a])]] if a in PLANE else x
@@ -182,41 +183,44 @@
             shuffled = jnp.take_along_axis(y, where, axis=1)
             term = strength_ref[a] * shuffled + drive_ref[section, a] * y
             out = out + (term if a in PLANE else flip_rows(term, ROW_BIT[a]))
-        side[2][i] = out
-
-    def tasks(number):
-        if number >= len(GROUPS):
-            return []
+        lead_ref[i] = out
+
+    def lefts(number):
+        section, places = GROUPS[number]
+        count = len(places)
+        side = sides[number % 2]
+        return [functools.partial(left, section, p, i, count, side) for i, p in enumerate(places)]
+
+    def combine(number):
         section, places = GROUPS[number]
         side = sides[number % 2]
-        made = []
-        for i, p in enumerate(places):
-            made.append(functools.partial(left, section, ORDER[p], i, side))
-            made.append(functools.partial(lead, section, ORDER[p], i, side))
-        return made
-
-    def combine(number, beside):
-        section, places = GROUPS[number]
-        high, low, leads = sides[number % 2]
         count = len(places)
+        beside = [functools.partial(lead, section, p, i) for i, p in enumerate(places)]
+        if number + 1 < len(GROUPS) - 1:
+            ahead = lefts(number + 1)
+            beside = [t for pair in itertools.zip_longest(beside, ahead) for t in pair if t is not None]
         dot = functools.partial(jnp.dot, preferred_element_type=f32)
-        out = None
+        half = count * ROWS
+        main = extra = None
         done = 0
         for k in range(KINDS):
             at = slice(k * TWO, (k + 1) * TWO)
-            rows = slice(0, count * ROWS)
-            part = dot(high[rows, at], high_w[at, :])
-            out = part if out is None else out + part
-            out = out + dot(low[rows, at], high_w[at, :])
-            out = out + dot(high[rows, at], low_w[at, :])
+            if number == 0 and k + 1 < KINDS:
+                split(k + 1)
+            part = dot(side[0 : 2 * half, at], high_w[at, :])
+            main = part if main is None else main + part
+            part = dot(side[0:half, at], low_w[at, :])
+            extra = part if extra is None else extra + part
             while done * KINDS < len(beside) * (k + 1):
                 beside[done]()
                 done += 1
         ahead = (0.5, 0.5, 1.0, 0.0)[section] * STEP_SIZE
         share = (1.0, 2.0, 2.0, 1.0)[section] * STEP_SIZE / 6.0
         for i, p in enumerate(places):
-            h_real = out[i * ROWS : (i + 1) * ROWS, :COLS] + leads[i, :ROWS]
-            h_imag = out[i * ROWS : (i + 1) * ROWS, COLS:] + leads[i, ROWS:]
+            rows = slice(i * ROWS, (i + 1) * ROWS)
+            out = main[rows] + main[half + i * ROWS : half + (i + 1) * ROWS] + extra[rows]
+            h_real = out[:, :COLS] + lead_ref[i, :ROWS]
+            h_imag = out[:, COLS:] + lead_ref[i, ROWS:]
             if section < 3:
                 states[section + 1][p, :ROWS] = state_one[p, :ROWS] + ahead * h_imag
                 states[section + 1][p, ROWS:] = state_one[p, ROWS:] - ahead * h_real
@@ -231,16 +235,15 @@
                     out_ref[:, 0, 0:COLS] = new_real
                     out_ref[:, 0, COLS:TWO] = new_imag
 
-    for task in tasks(0):
+    for task in lefts(0):
         task()
     copy.wait()
-    split()
+    split(0)
     for number in range(len(GROUPS)):
-        beside = tasks(number + 1)
-        early = len(beside) if number < 4 else 2 if number == 4 else 0
-        combine(number, beside[:early])
-        for task in beside[early:]:
-            task()
+        combine(number)
+        if number == len(GROUPS) - 2:
+            for task in lefts(number + 1):
+                task()
 
 
 def body(amplitudes, couplings, block_index, bond_map, bond_strength, drive_amplitude):
@@ -253,10 +256,15 @@
     sent = pl.pallas_call(
         prep_kernel,
         out_shape=jax.ShapeDtypeStruct((ROWS, 1, TWO + COLS), f32),
-        in_specs=[smem, vmem],
+        in_specs=[pl.BlockSpec(memory_space=pltpu.HBM)] * 2,
         out_specs=vmem,
+        scratch_shapes=[
+            pltpu.SMEM((ROWS // BROWS,), jnp.int32),
+            pltpu.VMEM((2, ROWS, COLS), f32),
+            pltpu.SemaphoreType.DMA((2,)),
+        ],
         compiler_params=small,
-    )(block_index, amplitudes)
+    )(*(pltpu.with_memory_space_constraint(array, pltpu.HBM) for array in (block_index, amplitudes)))
     held = lax.all_to_all(sent, line, 0, 0, tiled=True)
     copies = pl.pallas_call(
         pack_kernel,
@@ -285,8 +293,8 @@
             pltpu.VMEM((wide, TWO), bf16),
             pltpu.VMEM((wide, TWO), bf16),
         ]
-        + [pltpu.VMEM((MOST * ROWS, wide), bf16)] * 4
-        + [pltpu.VMEM((MOST, 2 * ROWS, COLS), f32)] * 2
+        + [pltpu.VMEM((2 * MOST * ROWS, wide), bf16)] * 2
+        + [pltpu.VMEM((MOST, 2 * ROWS, COLS), f32)]
         + [pltpu.VMEM((2 * ROWS, COLS), f32)],
         compiler_params=pltpu.CompilerParams(vmem_limit_bytes=32 << 20),
     )(bond_map, bond_strength, drive_amplitude, gathered, couplings)

time: 130 us -> 126 us (0.969)
  Pallas kernels: 17 us -> 14.9 us
  local copies, waits for them, and re-layouts: 1.52 us -> 0.02 us
    pallas_call x1, Pallas kernels: 15.7 us -> 13.2 us  [body(): pl.pallas_call(step_kernel, out_shape=jax.ShapeDtypeStruct((ROWS, 1, TWO)...]
    unnamed x12 -> x8, local copies, waits for them, and re-layouts: 1.52 us -> 0.02 us
where the time goes in v3:
time: 126 us
  blocking collectives  111 us (88%)
  Pallas kernels  14.9 us (12%)
    all_to_all x1, blocking collectives, body(): held = lax.all_to_all(sent, line, 0, 0, tiled=True)  56.3 us
    all_to_all x1, blocking collectives, body(): back = lax.all_to_all(result, line, 0, 0, tiled=True)  30.7 us
    all_to_all x1, blocking collectives, body(): gathered = lax.all_to_all(copies, 'plane', 0, 0, tiled=True)  24.1 us
    pallas_call x1, Pallas kernels, body(): pl.pallas_call(step_kernel, out_shape=jax.ShapeDtypeStruct((ROWS, 1, TWO)...  13.2 us

profile of v3, /device:TPU:1, one launch (start us, length us, event | category | flops | bytes accessed | tf_op | source)
XLA Modules:
  0.0 126.2 jit_solution(4719690448639294070)
XLA Ops:
  0.0 0.9 shard_map.64
  0.9 56.3 %all_to_all.15.in_ref = f32[64,1,384]{2,1,0:T(1,128)S(1)} all-to-all(f32[64,1,384]{2,1,0:T(1,128)S(1)} %shard_map.64), channel_id=1, replica_groups=mesh['grp'=16,'plane'=16,'far'=4] {'grp','far'}, dimensions={0} | all-to-all | bytes 196608 | tf_op jit(solution)/shard_map/all_to_all | solution.py:268
  57.3 0.1 shard_map.65
  57.4 0.0 copy-start
  57.4 0.0 copy-start.1
  57.4 0.0 copy-start.2
  57.4 0.0 copy-start.3
  57.4 24.1 %all_to_all.16.gathered_ref = f32[16,136,128]{2,1,0:T(8,128)S(1)} all-to-all(f32[16,136,128]{2,1,0:T(8,128)S(1)} %shard_map.65), channel_id=1, replica_groups=mesh['grp'=16,'plane'=16,'far'=4] {'plane'}, dimensions={0} | all-to-all | bytes 2228224 | tf_op jit(solution)/shard_map/all_to_all | solution.py:276
  81.6 0.0 copy-done
  81.6 0.0 copy-done.1
  81.6 0.0 copy-done.2
  81.6 0.0 copy-done.3
  81.6 13.2 %shard_map.66 = f32[64,1,256]{2,1,0:T(1,128)S(1)} custom-call(s32[10]{0:T(128)S(1)} %copy-done.2, f32[10]{0:T(128)S(1)} %copy-done.3, f32[4,10]{1,0:T(4,128)S(1)} %copy-done.1, f32[16,136,128]{2,1,0:T(8,128)S(1)} %all_to_all.16.gathered_ref, f32[2,12,128,128]{3,2,1,0:T(8,128)S(1)} %copy-done), custom_call_target="tpu_custom_call" | custom-call | tf_op jit(solution)/shard_map/pallas_call | solution.py:278
  94.8 30.7 %all_to_all.17.in_ref = f32[64,1,256]{2,1,0:T(1,128)S(1)} all-to-all(f32[64,1,256]{2,1,0:T(1,128)S(1)} %shard_map.66), channel_id=1, replica_groups=mesh['grp'=16,'plane'=16,'far'=4] {'grp','far'}, dimensions={0} | all-to-all | bytes 131072 | tf_op jit(solution)/shard_map/all_to_all | solution.py:301
  125.5 0.7 shard_map.67
Async XLA Ops:
  57.4 24.2 %copy-start = (f32[2,12,128,128]{3,2,1,0:T(8,128)S(1)}, f32[2,12,128,128]{3,2,1,0:T(8,128)}, u32[]{:S(2)}) copy-start(f32[2,12,128,128]{3,2,1,0:T(8,128)} %couplings_hbm.1) | copy-start | bytes 4718596
  57.4 24.2 %copy-start.1 = (f32[4,10]{1,0:T(4,128)S(1)}, f32[4,10]{1,0:T(4,128)}, u32[]{:S(2)}) copy-start(f32[4,10]{1,0:T(4,128)} %drive_ref.1) | copy-start | bytes 484
  57.4 24.2 %copy-start.2 = (s32[10]{0:T(128)S(1)}, s32[10]{0:T(128)}, u32[]{:S(2)}) copy-start(s32[10]{0:T(128)} %bond_ref.1) | copy-start | bytes 124
  57.4 24.2 %copy-start.3 = (f32[10]{0:T(128)S(1)}, f32[10]{0:T(128)}, u32[]{:S(2)}) copy-start(f32[10]{0:T(128)} %strength_ref.1) | copy-start | bytes 124
